TPU v7x, 32 devices: a whole 2x2x4 slice. The times are simulated.
32 devices in a mesh: seq: 8 (over z, y), head: 4 (over x, core).
Axes of the slice: x: 2, y: 2, z: 4, core: 2. Of those that a mesh axis runs over, the one named last changes fastest.
Arguments:
- queries: bfloat16 [2048, 1024], P('seq', 'head'), may hold values from -8 to 8
- key_rows: bfloat16 [2048, 1024], P('seq', 'head'), may hold values from -8 to 8
- value_rows: bfloat16 [2048, 1024], P('seq', 'head'), may hold values from -6 to 6
- attn_out_grad: bfloat16 [2048, 1024], P('seq', 'head'), may hold values from -6 to 6
- ssm_input: bfloat16 [2048, 512], P('seq', 'head'), may hold values from -6 to 6
- b_matrix: bfloat16 [2048, 256], P('seq'), may hold values from -2 to 2
- c_matrix: bfloat16 [2048, 256], P('seq'), may hold values from -2 to 2
- step_sizes: float32 [2048, 8], P('seq', 'head'), may hold values from 0.005 to 0.05
- decay_rates: float32 [8], P('head'), may hold values from 0.00024414062 to 0.5
- skip_gain: float32 [8], P('head'), may hold values from 0.5 to 1.5
- ssm_out_grad: bfloat16 [2048, 512], P('seq', 'head'), may hold values from -6 to 6
- doc_lengths: int32 [8], replicated, may hold values from 1 to 512, 2048 in all
Outputs:
- attn_out: bfloat16 [2048, 1024], P('seq', 'head')
- query_grad: bfloat16 [2048, 1024], P('seq', 'head')
- key_grad: bfloat16 [2048, 1024], P('seq', 'head')
- value_grad: bfloat16 [2048, 1024], P('seq', 'head')
- ssm_out: bfloat16 [2048, 512], P('seq', 'head')
- input_grad: bfloat16 [2048, 512], P('seq', 'head')
- b_grad: float32 [2048, 256], P('seq')
- c_grad: float32 [2048, 256], P('seq')
All inputs are finite; a program needn't handle non-finite values.
Results may differ from a plain program's by a relative error of at most 0.022.
Values may be sent and summed in bfloat16 or wider, within the bound.
No kernel may reach another device: no remote copies, remote signals or barrier semaphores. Data moves between devices by JAX's collectives and lax.ppermute only.
A program may use at most 128 MiB of HBM per device.

v0:
```python
import jax
import jax.numpy as jnp
from jax import lax
from jax.sharding import PartitionSpec as P

HEAD_DIM = 128
REACH = 2


def shifted(x, axis, by):
    length = lax.axis_size(axis)
    pairs = [(i, i + by) for i in range(length) if 0 <= i + by < length]
    return lax.ppermute(x, axis, pairs)


def entering(value, axis, join, neutral, backward):
    count, mine = (lax.axis_size(axis), lax.axis_index(axis))
    pieces = jax.tree.map(lambda part: lax.all_gather(part, axis), value)
    if backward:
        pieces = jax.tree.map(lambda part: part[::-1], pieces)
        mine = count - 1 - mine
    subtotal = jax.tree.map(
        lambda part, zero: jnp.full_like(part, 0) + jnp.asarray(zero, part.dtype), value, neutral
    )

    def lap(position, subtotal):
        longer = join(subtotal, jax.tree.map(lambda part: part[position], pieces))
        return jax.tree.map(lambda new, old: jnp.where(position < mine, new, old), longer, subtotal)

    return lax.fori_loop(0, count - 1, lap, subtotal)


def doc_index(positions, doc_ends):
    return jnp.sum((positions[:, None] >= doc_ends[None, :]).astype(jnp.int32), axis=1)


def visible_mask(query_pos, key_pos, doc_ends):
    same_doc = doc_index(query_pos, doc_ends)[:, None] == doc_index(key_pos, doc_ends)[None, :]
    return same_doc & (key_pos[None, :] <= query_pos[:, None]) & (key_pos[None, :] >= 0)


def split_heads(block_rows, head_width):
    return block_rows.reshape(block_rows.shape[0], -1, head_width)


def tile_reaches(query_first, key_last, doc_starts):
    opening = jnp.max(jnp.where(doc_starts <= query_first, doc_starts, 0))
    return opening <= key_last


def run_tile(reaches, work, running):
    return lax.cond(reaches, work, lambda unchanged: unchanged, running)


def scores_of(query_heads, key_heads, tile_mask):
    scores = jnp.einsum(
        "thd,shd->hts", query_heads, key_heads, preferred_element_type=jnp.float32
    ) * HEAD_DIM ** (-0.5)
    return jnp.where(tile_mask[None], scores, -jnp.inf)


def probabilities(scores, tile_mask, row_top, row_total):
    return jnp.where(
        tile_mask[None], jnp.exp(scores - row_top[:, :, None]) / row_total[:, :, None], 0.0
    )


def tile_slopes(
    query_heads, key_heads, value_heads, grad_heads, tile_mask, row_top, row_total, row_delta
):
    tile_probs = probabilities(
        scores_of(query_heads, key_heads, tile_mask), tile_mask, row_top, row_total
    )
    prob_grad = jnp.einsum(
        "thd,shd->hts", grad_heads, value_heads, preferred_element_type=jnp.float32
    )
    dscore = (tile_probs * (prob_grad - row_delta[:, :, None]) * HEAD_DIM ** (-0.5)).astype(
        jnp.bfloat16
    )
    return (tile_probs.astype(jnp.bfloat16), dscore)


def attention(queries, key_rows, value_rows, attn_out_grad, doc_ends, doc_starts):
    row_count = queries.shape[0]
    query_pos = lax.axis_index("seq") * row_count + jnp.arange(row_count, dtype=jnp.int32)
    query_heads = split_heads(queries, HEAD_DIM)
    grad_heads = split_heads(attn_out_grad, HEAD_DIM)
    key_heads = split_heads(key_rows, HEAD_DIM)
    value_heads = split_heads(value_rows, HEAD_DIM)
    head_count = query_heads.shape[1]
    blocks = [(key_heads, value_heads, query_pos)]
    for distance in range(1, REACH + 1):
        far_keys, far_values = shifted((key_rows, value_rows), "seq", distance)
        blocks.append(
            (
                split_heads(far_keys, HEAD_DIM),
                split_heads(far_values, HEAD_DIM),
                query_pos - distance * row_count,
            )
        )
    tile_masks = [visible_mask(query_pos, entry[2], doc_ends) for entry in blocks]
    reaches = [tile_reaches(query_pos[0], entry[2][-1], doc_starts) for entry in blocks]
    softmax_stats = (
        jnp.full((head_count, row_count), -jnp.inf, jnp.float32),
        jnp.zeros((head_count, row_count), jnp.float32),
    )
    for tile_index in range(len(blocks)):

        def grow_stats(running, key_block=blocks[tile_index][0], tile_mask=tile_masks[tile_index]):
            row_top, row_total = running
            scores = scores_of(query_heads, key_block, tile_mask)
            new_top = jnp.maximum(row_top, jnp.max(scores, axis=-1))
            new_total = row_total * jnp.exp(row_top - new_top) + jnp.sum(
                jnp.exp(scores - new_top[:, :, None]), axis=-1
            )
            return (new_top, new_total)

        if tile_index == 0:
            softmax_stats = grow_stats(softmax_stats)
        else:
            softmax_stats = run_tile(reaches[tile_index], grow_stats, softmax_stats)
    row_top, row_total = softmax_stats
    weighted = jnp.zeros((row_count, head_count, HEAD_DIM), jnp.float32)
    for tile_index in range(len(blocks)):

        def spread(running, key_block=blocks[tile_index], tile_mask=tile_masks[tile_index]):
            tile_probs = probabilities(
                scores_of(query_heads, key_block[0], tile_mask), tile_mask, row_top, row_total
            ).astype(jnp.bfloat16)
            return running + jnp.einsum(
                "hts,shd->thd", tile_probs, key_block[1], preferred_element_type=jnp.float32
            )

        if tile_index == 0:
            weighted = spread(weighted)
        else:
            weighted = run_tile(reaches[tile_index], spread, weighted)
    attn_rows = weighted.astype(jnp.bfloat16)
    row_delta = jnp.sum(grad_heads.astype(jnp.float32) * attn_rows.astype(jnp.float32), axis=-1).T
    probs_low, dscore = tile_slopes(
        query_heads,
        key_heads,
        value_heads,
        grad_heads,
        tile_masks[0],
        row_top,
        row_total,
        row_delta,
    )
    query_acc = jnp.einsum("hts,shd->thd", dscore, key_heads, preferred_element_type=jnp.float32)
    key_acc = jnp.einsum("hts,thd->shd", dscore, query_heads, preferred_element_type=jnp.float32)
    value_acc = jnp.einsum(
        "hts,thd->shd", probs_low, grad_heads, preferred_element_type=jnp.float32
    )
    zero_keys = jnp.zeros((row_count, head_count, HEAD_DIM), jnp.float32)
    for tile_index in range(1, len(blocks)):

        def slope_tile(running, key_block=blocks[tile_index], tile_mask=tile_masks[tile_index]):
            tile_low, tile_dscore = tile_slopes(
                query_heads,
                key_block[0],
                key_block[1],
                grad_heads,
                tile_mask,
                row_top,
                row_total,
                row_delta,
            )
            query_part = running[0] + jnp.einsum(
                "hts,shd->thd", tile_dscore, key_block[0], preferred_element_type=jnp.float32
            )
            key_part = jnp.einsum(
                "hts,thd->shd", tile_dscore, query_heads, preferred_element_type=jnp.float32
            )
            value_part = jnp.einsum(
                "hts,thd->shd", tile_low, grad_heads, preferred_element_type=jnp.float32
            )
            return (query_part, key_part, value_part)

        query_acc, key_part, value_part = run_tile(
            reaches[tile_index], slope_tile, (query_acc, zero_keys, zero_keys)
        )
        back_keys, back_values = shifted((key_part, value_part), "seq", -tile_index)
        key_acc = key_acc + back_keys
        value_acc = value_acc + back_values
    return (
        attn_rows.reshape(row_count, -1),
        query_acc.astype(jnp.bfloat16).reshape(row_count, -1),
        key_acc.astype(jnp.bfloat16).reshape(row_count, -1),
        value_acc.astype(jnp.bfloat16).reshape(row_count, -1),
    )


def ssm_parts(x_heads, b_rows, intersection, step_sizes, decay_rates, skip_gain):
    row_count = x_heads.shape[0]
    offsets = jnp.arange(row_count, dtype=jnp.int32)
    log_decay = jnp.cumsum(-step_sizes * decay_rates[None, :], axis=0)
    causal = offsets[None, :] <= offsets[:, None]
    log_gaps = log_decay.T[:, :, None] - log_decay.T[:, None, :]
    fading = jnp.where(causal[None], jnp.exp(jnp.where(causal[None], log_gaps, 0.0)), 0.0)
    mixing = intersection[None] * fading * step_sizes.T[:, None, :]
    direct = jnp.einsum("hts,shp->thp", mixing, x_heads, precision=lax.Precision.HIGHEST)
    direct = direct + skip_gain[None, :, None] * x_heads
    carry_weight = jnp.exp(log_decay)
    tail_weight = jnp.exp(log_decay[-1][None, :] - log_decay) * step_sizes
    local_state = jnp.einsum(
        "th,tn,thp->hnp", tail_weight, b_rows, x_heads, precision=lax.Precision.HIGHEST
    )
    decay_all = jnp.exp(log_decay[-1])
    return (direct, local_state, decay_all, carry_weight)


def chained(earlier, later_item):
    return (earlier[0] * later_item[0], later_item[0][:, None, None] * earlier[1] + later_item[1])


def ssm_layer(ssm_input, b_matrix, c_matrix, step_sizes, decay_rates, skip_gain, ssm_out_grad):
    row_count = ssm_input.shape[0]
    head_count = decay_rates.shape[0]
    x_heads = ssm_input.astype(jnp.float32).reshape(row_count, head_count, -1)
    b_rows = b_matrix.astype(jnp.float32)
    c_rows = c_matrix.astype(jnp.float32)
    intersection = jnp.dot(c_matrix, b_matrix.T, preferred_element_type=jnp.float32)

    def local_terms(x_value, b_value, intersection_value):
        return ssm_parts(x_value, b_value, intersection_value, step_sizes, decay_rates, skip_gain)

    (direct, local_state, decay_all, carry_weight), pullback = jax.vjp(
        local_terms, x_heads, b_rows, intersection
    )
    identity = (jnp.ones_like(decay_all), jnp.zeros_like(local_state))
    state_in = entering((decay_all, local_state), "seq", chained, identity, False)[1]
    incoming = jnp.einsum("tn,hnp->thp", c_rows, state_in, precision=lax.Precision.HIGHEST)
    ssm_rows = direct + carry_weight[:, :, None] * incoming
    grad_heads = ssm_out_grad.astype(jnp.float32).reshape(row_count, head_count, -1)
    adjoint = jnp.einsum(
        "th,tn,thp->hnp", carry_weight, c_rows, grad_heads, precision=lax.Precision.HIGHEST
    )
    adjoint_in = entering((decay_all, adjoint), "seq", chained, identity, True)[1]
    weight_grad = jnp.sum(grad_heads * incoming, axis=-1)
    x_grad, b_grad, intersection_grad = pullback(
        (grad_heads, adjoint_in, jnp.zeros_like(decay_all), weight_grad)
    )
    b_grad = b_grad + jnp.dot(intersection_grad.T, c_rows, precision=lax.Precision.HIGHEST)
    c_grad = jnp.dot(intersection_grad, b_rows, precision=lax.Precision.HIGHEST)
    c_grad = c_grad + jnp.einsum(
        "th,thp,hnp->tn", carry_weight, grad_heads, state_in, precision=lax.Precision.HIGHEST
    )
    b_grad, c_grad = lax.psum((b_grad, c_grad), "head")
    return (
        ssm_rows.reshape(row_count, -1).astype(jnp.bfloat16),
        x_grad.reshape(row_count, -1).astype(jnp.bfloat16),
        b_grad,
        c_grad,
    )


def on_device(
    queries,
    key_rows,
    value_rows,
    attn_out_grad,
    ssm_input,
    b_matrix,
    c_matrix,
    step_sizes,
    decay_rates,
    skip_gain,
    ssm_out_grad,
    doc_lengths,
):
    doc_ends = jnp.cumsum(doc_lengths, dtype=jnp.int32)
    doc_starts = doc_ends - doc_lengths
    attn_out, query_grad, key_grad, value_grad = attention(
        queries, key_rows, value_rows, attn_out_grad, doc_ends, doc_starts
    )
    ssm_out, input_grad, b_grad, c_grad = ssm_layer(
        ssm_input, b_matrix, c_matrix, step_sizes, decay_rates, skip_gain, ssm_out_grad
    )
    return (attn_out, query_grad, key_grad, value_grad, ssm_out, input_grad, b_grad, c_grad)


def solution(mesh):
    in_specs = (
        P("seq", "head"),
        P("seq", "head"),
        P("seq", "head"),
        P("seq", "head"),
        P("seq", "head"),
        P("seq", None),
        P("seq", None),
        P("seq", "head"),
        P("head"),
        P("head"),
        P("seq", "head"),
        P(),
    )
    out_specs = (
        P("seq", "head"),
        P("seq", "head"),
        P("seq", "head"),
        P("seq", "head"),
        P("seq", "head"),
        P("seq", "head"),
        P("seq", None),
        P("seq", None),
    )
    return jax.shard_map(
        on_device, mesh=mesh, in_specs=in_specs, out_specs=out_specs, check_vma=False
    )
```

profile of v0, /device:TPU:0, one launch (start us, length us, event | category | flops | bytes accessed | tf_op | source)
XLA Modules:
  0.0 176.5 jit_solution(7629015517611655962)
XLA Ops:
  11.6 1.8 %convolution_bitcast_fusion.16 = f32[2,256,64]{1,2,0:T(8,128)} fusion(bf16[256,2,64]{0,2,1:T(8,128)(2,1)S(1)} %bitcast.249, bf16[256,256]{1,0:T(8,128)(2,1)} %param.34, f32[256,2]{0,1:T(2,128)S(1)} %get-tuple-element.661), kind=kOutput, calls=%fused_computation.116 | convolution fusion | flops 100728832 | bytes 329728 | tf_op jit(solution)/shard_map/th,tn,thp->hnp/dot_general | solution.py:236
  14.5 4.9 %collective-permute-start = (bf16[256,256]{0,1:T(8,128)(2,1)S(1)}, bf16[256,256]{0,1:T(8,128)(2,1)S(1)}, u32[]{:S(2)}, u32[]{:S(2)}) collective-permute-start(bf16[256,256]{0,1:T(8,128)(2,1)S(1)} %copy.215), channel_id=1, source_target_pairs={{0,4},{4,8},{8,12},{12,16},{16,20},{20,24},{24,28},{1,5},{5,9},{9,... | collective-permute-start | bytes 393224 | tf_op jit(solution)/shard_map/ppermute | solution.py:13
  19.4 3.5 %collective-permute-start.1 = (bf16[256,256]{0,1:T(8,128)(2,1)S(1)}, bf16[256,256]{0,1:T(8,128)(2,1)S(1)}, u32[]{:S(2)}, u32[]{:S(2)}) collective-permute-start(bf16[256,256]{0,1:T(8,128)(2,1)S(1)} %copy.215), channel_id=1, source_target_pairs={{0,8},{4,12},{8,16},{12,20},{16,24},{20,28},{1,9},{5,13},{9,17},{1... | collective-permute-start | bytes 393224 | tf_op jit(solution)/shard_map/ppermute | solution.py:13
  23.9 3.4 %collective-permute-start.2 = (bf16[256,256]{0,1:T(8,128)(2,1)S(1)}, bf16[256,256]{0,1:T(8,128)(2,1)S(1)}, u32[]{:S(2)}, u32[]{:S(2)}) collective-permute-start(bf16[256,256]{0,1:T(8,128)(2,1)S(1)} %copy.225), channel_id=1, source_target_pairs={{0,4},{4,8},{8,12},{12,16},{16,20},{20,24},{24,28},{1,5},{5,9},{9,... | collective-permute-start | bytes 393224 | tf_op jit(solution)/shard_map/ppermute | solution.py:13
  27.4 3.5 %collective-permute-start.3 = (bf16[256,256]{0,1:T(8,128)(2,1)S(1)}, bf16[256,256]{0,1:T(8,128)(2,1)S(1)}, u32[]{:S(2)}, u32[]{:S(2)}) collective-permute-start(bf16[256,256]{0,1:T(8,128)(2,1)S(1)} %copy.225), channel_id=1, source_target_pairs={{0,8},{4,12},{8,16},{12,20},{16,24},{20,28},{1,9},{5,13},{9,17},{1... | collective-permute-start | bytes 393224 | tf_op jit(solution)/shard_map/ppermute | solution.py:13
  32.9 1.1 fusion.122
  36.9 1.3 fusion.115
  41.0 1.2 fusion.77
  42.6 1.8 %conditional.14 = (bf16[256,2,128]{0,2,1:T(8,128)(2,1)}, bf16[256,256]{1,0:T(8,128)(2,1)S(1)}) conditional(s32[]{:T(128)} %convert_element_type.92, (f32[256,2,128]{2,0,1:T(8,128)S(1)}) %conditional.13, (pred[256,256]{1,0:T(8,128)(4,1)S(1)}, bf16[256,2,128]{0,2,1:T(8,128)(2,1)S(1)}, bf16[256,2,128]{0,2,1:T(8,128)(2,1)S(1)}, ...), branch_computations={%region_17.18_spmd, %region_18.19_spmd} | conditional | flops 68026368 | bytes 1642512
  46.2 1.3 collective-permute-start.7
  47.7 1.3 collective-permute-start.6
  49.0 1.1 fusion.65
  50.2 27.2 %all-gather.2 = f32[8,1,2]{2,1,0:T(1,128)S(1)} all-gather(f32[1,1,2]{2,1,0:T(1,128)S(1)} %bitcast.286), channel_id=1, replica_groups=mesh['seq'=8,'head'=4] {'seq'}, dimensions={0}, use_global_device_ids=true | all-gather | bytes 72 | tf_op jit(solution)/shard_map/all_gather | solution.py:18
  79.7 1.3 collective-permute-start.5
  81.2 1.5 collective-permute-start.4
  83.3 1.3 fusion.71
  85.4 8.9 %collective-permute-done.5 = f32[256,2,128]{0,2,1:T(8,128)} collective-permute-done((f32[256,2,128]{0,2,1:T(8,128)}, f32[256,2,128]{0,2,1:T(8,128)}, u32[]{:S(2)}, u32[]{:S(2)}) %collective-permute-start.5) | collective-permute-done | bytes 262176 | tf_op jit(solution)/shard_map/ppermute | solution.py:13
  94.3 1.2 fusion.70
  96.2 1.8 %copy.263 = f32[8,2,256,64]{3,2,1,0:T(8,128)S(1)} copy(f32[8,2,256,64]{2,3,1,0:T(8,128)} %bitcast.248) | data formatting | bytes 2097152 | tf_op jit(solution)/shard_map/all_gather | solution.py:18
  98.1 1.5 rev.7
  99.5 12.3 %while.29 = (s32[]{:T(128)}, f32[2,256,64]{2,1,0:T(8,128)S(1)}, s32[]{:T(128)}, f32[8,2]{1,0:T(8,128)}, f32[8,2,256,64]{3,2,1,0:T(8,128)}, /*index=5*/s32[]{:T(128)}, s32[]{:T(128)}) while((s32[]{:T(128)}, f32[2,256,64]{2,1,0:T(8,128)S(1)}, s32[]{:T(128)}, f32[8,2]{1,0:T(8,128)}, f32[8,2,256,64]{3,2,1,0:T(8,128)}, ...), condition=%wide.region_29.30_spmd.clone, body=%wide.region_28.29_spmd.clone.sunk | while | flops 131076 | bytes 393345 | solution.py:30
  100.3 1.0 fusion.176
  102.0 1.0 fusion.176
  103.8 1.0 fusion.176
  105.5 1.0 fusion.176
  107.3 1.0 fusion.176
  110.8 1.0 fusion.176
  112.9 13.0 %while.28 = (s32[]{:T(128)}, f32[2,256,64]{2,1,0:T(8,128)S(1)}, s32[]{:T(128)}, f32[8,2]{1,0:T(8,128)}, f32[8,2,256,64]{2,3,1,0:T(8,128)}, /*index=5*/s32[]{:T(128)}, s32[]{:T(128)}) while((s32[]{:T(128)}, f32[2,256,64]{2,1,0:T(8,128)S(1)}, s32[]{:T(128)}, f32[8,2]{1,0:T(8,128)}, f32[8,2,256,64]{2,3,1,0:T(8,128)}, ...), condition=%wide.region_27.28_spmd.clone, body=%wide.region_26.27_spmd.clone.sunk | while | flops 131076 | bytes 917633 | solution.py:30
  127.6 1.1 convolution_add_fusion
  131.2 35.4 %all-reduce.3.cloned.1.call-done = (f32[256,256]{1,0:T(8,128)}, f32[256,256]{1,0:T(8,128)}) async-done(((f32[256,256]{1,0:T(8,128)}, f32[256,256]{1,0:T(8,128)}), (f32[256,256]{1,0:T(8,128)}, f32[256,256]{1,0:T(8,128)})) %all-reduce.3.cloned.1.call-update) | async-done | bytes 524304 | tf_op jit(solution)/shard_map/psum | solution.py:249
  166.6 1.7 copy.388
  168.3 1.7 copy.389
  (172 shorter events, 43.9 us)
Async XLA Ops:
  7.2 24.6 %copy-start = (bf16[256,256]{1,0:T(8,128)(2,1)S(1)}, bf16[256,256]{1,0:T(8,128)(2,1)}, u32[]{:S(2)}) copy-start(bf16[256,256]{1,0:T(8,128)(2,1)} %param.33) | copy-start | bytes 393220
  7.2 29.4 %copy-start.6 = (bf16[256,256]{1,0:T(8,128)(2,1)S(1)}, bf16[256,256]{1,0:T(8,128)(2,1)}, u32[]{:S(2)}) copy-start(bf16[256,256]{1,0:T(8,128)(2,1)} %param.29) | copy-start | bytes 393220
  7.2 28.6 %copy-start.24 = (s32[8]{0:T(128)S(1)}, s32[8]{0:T(128)}, u32[]{:S(2)}) copy-start(s32[8]{0:T(128)} %param.39) | copy-start | bytes 100
  7.2 29.3 %copy-start.9 = (bf16[256,256]{1,0:T(8,128)(2,1)S(1)}, bf16[256,256]{1,0:T(8,128)(2,1)}, u32[]{:S(2)}) copy-start(bf16[256,256]{1,0:T(8,128)(2,1)} %param.28) | copy-start | bytes 393220
  7.2 89.0 %all-gather.8.cloned.1.call-start = ((), (), s32[]{:S(2)}) async-start(), calls=%async_computation.1 | async-start | bytes 1179648 | tf_op jit(solution)/shard_map/all_gather | solution.py:18
  9.2 31.8 %copy-start.21 = (f32[1,2,2,128]{3,1,2,0:T(2,128)}, f32[1,2,2,128]{3,1,2,0:T(2,128)S(1)}, u32[]{:S(2)}) copy-start(f32[1,2,2,128]{3,1,2,0:T(2,128)S(1)} %copy.345) | copy-start | bytes 6148
  11.6 37.4 %copy-start.2 = (bf16[256,128]{0,1:T(8,128)(2,1)}, bf16[256,128]{0,1:T(8,128)(2,1)S(1)}, u32[]{:S(2)}) copy-start(bf16[256,128]{0,1:T(8,128)(2,1)S(1)} %copy.262) | copy-start | bytes 196612
  11.6 29.3 %copy-start.10 = (bf16[256,256]{1,0:T(8,128)(2,1)S(1)}, bf16[256,256]{1,0:T(8,128)(2,1)}, u32[]{:S(2)}) copy-start(bf16[256,256]{1,0:T(8,128)(2,1)} %param.31) | copy-start | bytes 393220
  13.4 27.5 %copy-start.19 = (f32[256,2]{0,1:T(2,128)S(1)}, f32[256,2]{0,1:T(2,128)}, u32[]{:S(2)}) copy-start(f32[256,2]{0,1:T(2,128)} %param.35) | copy-start | bytes 6148
  13.4 27.5 %copy-start.25 = (f32[2]{0:T(128)S(1)}, f32[2]{0:T(128)}, u32[]{:S(2)}) copy-start(f32[2]{0:T(128)} %param.37) | copy-start | bytes 28
  13.4 99.4 %all-gather.6.cloned.1.call-start = ((), (), s32[]{:S(2)}) async-start(), calls=%async_computation | async-start | bytes 1179648 | tf_op jit(solution)/shard_map/all_gather | solution.py:18
  14.5 27.7 %collective-permute-start = (bf16[256,256]{0,1:T(8,128)(2,1)S(1)}, bf16[256,256]{0,1:T(8,128)(2,1)S(1)}, u32[]{:S(2)}, u32[]{:S(2)}) collective-permute-start(bf16[256,256]{0,1:T(8,128)(2,1)S(1)} %copy.215), channel_id=1, source_target_pairs={{0,4},{4,8},{8,12},{12,16},{16,20},{20,24},{24,28},{1,5},{5,9},{9,... | collective-permute-start | bytes 393224 | tf_op jit(solution)/shard_map/ppermute | solution.py:13
  19.4 22.8 %collective-permute-start.1 = (bf16[256,256]{0,1:T(8,128)(2,1)S(1)}, bf16[256,256]{0,1:T(8,128)(2,1)S(1)}, u32[]{:S(2)}, u32[]{:S(2)}) collective-permute-start(bf16[256,256]{0,1:T(8,128)(2,1)S(1)} %copy.215), channel_id=1, source_target_pairs={{0,8},{4,12},{8,16},{12,20},{16,24},{20,28},{1,9},{5,13},{9,17},{1... | collective-permute-start | bytes 393224 | tf_op jit(solution)/shard_map/ppermute | solution.py:13
  23.9 18.6 %collective-permute-start.2 = (bf16[256,256]{0,1:T(8,128)(2,1)S(1)}, bf16[256,256]{0,1:T(8,128)(2,1)S(1)}, u32[]{:S(2)}, u32[]{:S(2)}) collective-permute-start(bf16[256,256]{0,1:T(8,128)(2,1)S(1)} %copy.225), channel_id=1, source_target_pairs={{0,4},{4,8},{8,12},{12,16},{16,20},{20,24},{24,28},{1,5},{5,9},{9,... | collective-permute-start | bytes 393224 | tf_op jit(solution)/shard_map/ppermute | solution.py:13
  27.4 15.2 %collective-permute-start.3 = (bf16[256,256]{0,1:T(8,128)(2,1)S(1)}, bf16[256,256]{0,1:T(8,128)(2,1)S(1)}, u32[]{:S(2)}, u32[]{:S(2)}) collective-permute-start(bf16[256,256]{0,1:T(8,128)(2,1)S(1)} %copy.225), channel_id=1, source_target_pairs={{0,8},{4,12},{8,16},{12,20},{16,24},{20,28},{1,9},{5,13},{9,17},{1... | collective-permute-start | bytes 393224 | tf_op jit(solution)/shard_map/ppermute | solution.py:13
  31.8 17.2 %copy-start.4 = (bf16[256,128]{0,1:T(8,128)(2,1)}, bf16[256,128]{0,1:T(8,128)(2,1)S(1)}, u32[]{:S(2)}) copy-start(bf16[256,128]{0,1:T(8,128)(2,1)S(1)} %copy.256) | copy-start | bytes 196612
  32.7 133.9 %all-reduce.3.cloned.1.call-start = ((), (), s32[]{:S(2)}) async-start(), calls=%async_computation.2 | async-start | bytes 1048576 | tf_op jit(solution)/shard_map/psum | solution.py:249
  32.9 9.3 %copy-start.14 = (pred[256,256]{0,1:T(8,128)(4,1)}, pred[256,256]{0,1:T(8,128)(4,1)S(1)}, u32[]{:S(2)}) copy-start(pred[256,256]{0,1:T(8,128)(4,1)S(1)} %iota_compare_fusion) | copy-start | bytes 196612
  34.0 8.1 %copy-start.7 = (f32[256,256]{0,1:T(8,128)}, f32[256,256]{0,1:T(8,128)S(1)}, u32[]{:S(2)}) copy-start(f32[256,256]{0,1:T(8,128)S(1)} %fusion.122) | copy-start | bytes 786436
  36.5 8.9 %copy-start.17 = (pred[256,256]{0,1:T(8,128)(4,1)}, pred[256,256]{0,1:T(8,128)(4,1)S(1)}, u32[]{:S(2)}) copy-start(pred[256,256]{0,1:T(8,128)(4,1)S(1)} %copy.211) | copy-start | bytes 196612
  46.0 3.0 %copy-start.15 = (pred[256,256]{0,1:T(8,128)(4,1)S(1)}, pred[256,256]{0,1:T(8,128)(4,1)}, u32[]{:S(2)}) copy-start(pred[256,256]{0,1:T(8,128)(4,1)} %copy-done.14) | copy-start | bytes 196612
  46.1 4.1 %copy-start.23 = (f32[2]{0:T(128)S(1)}, f32[2]{0:T(128)}, u32[]{:S(2)}) copy-start(f32[2]{0:T(128)} %get-tuple-element.631) | copy-start | bytes 28
  46.1 37.2 %copy-start.18 = (pred[256,256]{0,1:T(8,128)(4,1)S(1)}, pred[256,256]{0,1:T(8,128)(4,1)}, u32[]{:S(2)}) copy-start(pred[256,256]{0,1:T(8,128)(4,1)} %copy-done.17) | copy-start | bytes 196612
  46.2 37.1 %collective-permute-start.7 = (f32[256,2,128]{0,2,1:T(8,128)S(1)}, f32[256,2,128]{0,2,1:T(8,128)}, u32[]{:S(2)}, u32[]{:S(2)}) collective-permute-start(f32[256,2,128]{0,2,1:T(8,128)S(1)} %copy.254), channel_id=1, source_target_pairs={{8,0},{12,4},{16,8},{20,12},{24,16},{28,20},{9,1},{13,5},{17,9},{2... | collective-permute-start | bytes 786440 | tf_op jit(solution)/shard_map/ppermute | solution.py:13
  47.7 35.6 %collective-permute-start.6 = (f32[256,2,128]{0,2,1:T(8,128)S(1)}, f32[256,2,128]{0,2,1:T(8,128)}, u32[]{:S(2)}, u32[]{:S(2)}) collective-permute-start(f32[256,2,128]{0,2,1:T(8,128)S(1)} %copy.253), channel_id=1, source_target_pairs={{4,0},{8,4},{12,8},{16,12},{20,16},{24,20},{28,24},{5,1},{9,5},{13... | collective-permute-start | bytes 786440 | tf_op jit(solution)/shard_map/ppermute | solution.py:13
  79.7 14.5 %collective-permute-start.5 = (f32[256,2,128]{0,2,1:T(8,128)}, f32[256,2,128]{0,2,1:T(8,128)}, u32[]{:S(2)}, u32[]{:S(2)}) collective-permute-start(f32[256,2,128]{0,2,1:T(8,128)} %copy.251), channel_id=1, source_target_pairs={{8,0},{12,4},{16,8},{20,12},{24,16},{28,20},{9,1},{13,5},{17,9},{2... | collective-permute-start | bytes 786440 | tf_op jit(solution)/shard_map/ppermute | solution.py:13
  81.2 13.1 %collective-permute-start.4 = (f32[256,2,128]{0,2,1:T(8,128)S(1)}, f32[256,2,128]{0,2,1:T(8,128)S(1)}, u32[]{:S(2)}, u32[]{:S(2)}) collective-permute-start(f32[256,2,128]{0,2,1:T(8,128)S(1)} %copy.250), channel_id=1, source_target_pairs={{4,0},{8,4},{12,8},{16,12},{20,16},{24,20},{28,24},{5,1},{9,5},{13... | collective-permute-start | bytes 786440 | tf_op jit(solution)/shard_map/ppermute | solution.py:13
  99.5 12.3 %copy-start.5 = (bf16[256,128]{0,1:T(8,128)(2,1)S(1)}, bf16[256,128]{0,1:T(8,128)(2,1)}, u32[]{:S(2)}) copy-start(bf16[256,128]{0,1:T(8,128)(2,1)} %copy-done.4) | copy-start | bytes 196612
  99.5 12.9 %copy-start.3 = (bf16[256,128]{0,1:T(8,128)(2,1)S(1)}, bf16[256,128]{0,1:T(8,128)(2,1)}, u32[]{:S(2)}) copy-start(bf16[256,128]{0,1:T(8,128)(2,1)} %copy-done.2) | copy-start | bytes 196612
  99.5 12.9 %copy-start.26 = (f32[2]{0:T(128)S(1)}, f32[2]{0:T(128)}, u32[]{:S(2)}) copy-start(f32[2]{0:T(128)} %param.37) | copy-start | bytes 28
  112.9 13.7 %copy-start.1 = (bf16[256,256]{1,0:T(8,128)(2,1)S(1)}, bf16[256,256]{1,0:T(8,128)(2,1)}, u32[]{:S(2)}) copy-start(bf16[256,256]{1,0:T(8,128)(2,1)} %param.34) | copy-start | bytes 393220
  126.0 4.1 %copy-start.13 = (f32[256,2,64]{0,2,1:T(8,128)S(1)}, f32[256,2,64]{0,2,1:T(8,128)}, u32[]{:S(2)}) copy-start(f32[256,2,64]{0,2,1:T(8,128)} %fusion.77) | copy-start | bytes 393220
  (6 other events, 13.9 us)
Sparse Core Ops, SparseCore 0:
  13.6 44.8 all-gather.7
  60.6 41.7 all-gather.5
  128.8 37.7 all-reduce.2
where the time goes:
time: 176 us
  waiting for transfers between devices  44.4 us (25%)
  local copies, waits for them, and re-layouts  38.2 us (22%)
  blocking collectives  27.2 us (15%)
  starting transfers between devices  20.8 us (12%)
  between operations  17 us (10%)
  matrix products  14.3 us (8%)
  other arithmetic  14.2 us (8%)
    psum x1, waiting for transfers between devices, ssm_layer(): b_grad, c_grad = lax.psum((b_grad, c_grad), 'head')  35.4 us
    all_gather x1, blocking collectives, entering(): pieces = jax.tree.map(lambda part: lax.all_gather(part, axis), value)  27.2 us
    ppermute x8, starting transfers between devices, shifted(): return lax.ppermute(x, axis, pairs)  20.6 us
    unnamed x69, local copies, waits for them, and re-layouts  11.9 us
    mul x14, local copies, waits for them, and re-layouts, chained(): later_item[0][:, None, None] * earlier[1] + later_item[1]  9.66 us
    ppermute x8, waiting for transfers between devices, shifted(): return lax.ppermute(x, axis, pairs)  8.9 us
    select_n x14, other arithmetic, lap(): jnp.where(position < mine, new, old)  8.04 us
    dynamic_slice x14, local copies, waits for them, and re-layouts, lap(): longer = join(subtotal, jax.tree.map(lambda part: part[position], pieces))  7.32 us
  transfers between devices with their start and end apart: 11, of which 2 were waited for; matrix products, arithmetic and copies ran while one was open for 24% of the time, Pallas kernels for 0%

commit v1 on v0

v1 whole, which is shorter than its diff:
```python
import functools
import math

import jax
import jax.numpy as jnp
from jax import lax
from jax.experimental import pallas as pl
from jax.experimental.pallas import tpu as pltpu
from jax.sharding import PartitionSpec as P

HEAD_DIM = 128
REACH = 2
F32 = jnp.float32
BF16 = jnp.bfloat16
SCALE = HEAD_DIM ** (-0.5)
SCALE_LOG2E = SCALE * math.log2(math.e)
HIDDEN = -1e30

VMEM = pl.BlockSpec(memory_space=pltpu.VMEM)
SMEM = pl.BlockSpec(memory_space=pltpu.SMEM)


def mm(a, b):
    return lax.dot_general(a, b, (((1,), (0,)), ((), ())), preferred_element_type=F32)


def mm_nt(a, b):
    return lax.dot_general(a, b, (((1,), (1,)), ((), ())), preferred_element_type=F32)


def mm_tn(a, b):
    return lax.dot_general(a, b, (((0,), (0,)), ((), ())), preferred_element_type=F32)


def call(kernel, outs, in_specs, name, flops, *args, scratch=()):
    moved = sum(a.size * a.dtype.itemsize for a in args)
    moved += sum(math.prod(s) * jnp.dtype(d).itemsize for s, d in outs)
    return pl.pallas_call(
        kernel,
        out_shape=[jax.ShapeDtypeStruct(s, d) for s, d in outs],
        in_specs=in_specs,
        out_specs=[VMEM] * len(outs),
        scratch_shapes=list(scratch),
        name=name,
        cost_estimate=pl.CostEstimate(flops=flops, bytes_accessed=moved, transcendentals=0),
    )(*args)


def shifted(x, axis, by):
    length = lax.axis_size(axis)
    return lax.ppermute(x, axis, [(i, i + by) for i in range(length) if 0 <= i + by < length])


def swapped(x, axis, bit):
    return lax.ppermute(x, axis, [(i, i ^ bit) for i in range(lax.axis_size(axis))])


def by_head(shape, width, values):
    lane = lax.broadcasted_iota(jnp.int32, shape, 1)
    full = jnp.broadcast_to(values[0], shape)
    for h in range(1, len(values)):
        full = jnp.where(lane >= h * width, jnp.broadcast_to(values[h], shape), full)
    return full


def first_kernel(
    rate, q, k, v, do, x, g, b, c, dt, kv, qg, uv, msg, ew
):
    rows, cols = x.shape
    heads = dt.shape[1]
    width = cols // heads
    kv[:rows, :] = k[...]
    kv[rows:, :] = v[...]
    qg[:rows, :] = q[...]
    qg[rows:, :] = do[...]
    dts = by_head((rows, cols), width, [dt[:, h : h + 1] for h in range(heads)])
    lane = lax.broadcasted_iota(jnp.int32, (1, cols), 1)
    rates = jnp.full((1, cols), rate[0], F32)
    for h in range(1, heads):
        rates = jnp.where(lane >= h * width, rate[h], rates)
    logs = dts * (-rates)
    tri = (
        lax.broadcasted_iota(jnp.int32, (rows, rows), 1)
        <= lax.broadcasted_iota(jnp.int32, (rows, rows), 0)
    ).astype(F32).astype(BF16)
    high = logs.astype(BF16)
    rest = logs - high.astype(F32)
    mid = rest.astype(BF16)
    low = (rest - mid.astype(F32)).astype(BF16)
    total = mm(tri, high) + mm(tri, mid) + mm(tri, low)
    grow = jnp.exp(total)
    weight = dts * jnp.exp(-total)
    ew[:rows, :] = grow
    ew[rows:, :] = weight
    u = (weight * x[...].astype(F32)).astype(BF16)
    w = (grow * g[...].astype(F32)).astype(BF16)
    uv[:rows, :] = u
    uv[rows:, :] = w
    n = b.shape[1]
    state = mm_tn(u, b[...])
    ahead = mm_tn(w, c[...])
    row = lax.broadcasted_iota(jnp.int32, (16, n), 0)
    ends = jnp.zeros((16, n), F32)
    for h in range(heads):
        end = jnp.sum(dt[:, h : h + 1], axis=0, keepdims=True) * (-rate[h])
        end = jnp.broadcast_to(end, (1, n))
        ends = jnp.where(row == h, jnp.broadcast_to(end, (16, n)), ends)
        sl = slice(h * width, (h + 1) * width)
        msg[sl, :] = (state[sl, :] * jnp.exp(end)).astype(BF16)
    msg[cols : 2 * cols, :] = ahead.astype(BF16)
    top = ends.astype(BF16)
    msg[2 * cols : 2 * cols + 16, :] = top
    msg[2 * cols + 16 :, :] = (ends - top.astype(F32)).astype(BF16)


def decay_of(msg, cols):
    return msg[2 * cols : 2 * cols + 16, :].astype(F32) + msg[2 * cols + 16 :, :].astype(F32)


def join_kernel(heads, bit, first, last, mine, other, *refs):
    if first:
        sent, kept = refs
    else:
        held, sent, kept = refs
    cols = (mine.shape[0] - 32) // 2
    width = cols // heads
    index = lax.axis_index("seq")
    upper = (index & bit) != 0
    log_mine, log_other = decay_of(mine, cols), decay_of(other, cols)
    fade_mine, fade_other = jnp.exp(log_mine), jnp.exp(log_other)
    if first:
        log_before = log_after = jnp.zeros_like(log_mine)
    else:
        log_before = held[2 * cols : 2 * cols + 16, :]
        log_after = held[2 * cols + 16 :, :]
    before, after = jnp.exp(log_before), jnp.exp(log_after)
    low_fade = jnp.where(upper, fade_other, fade_mine)
    high_fade = jnp.where(upper, fade_mine, fade_other)
    next_upper = (index & (2 * bit)) != 0
    for h in range(heads):
        sl = slice(h * width, (h + 1) * width)
        al = slice(cols + h * width, cols + (h + 1) * width)
        s_mine, s_other = mine[sl, :].astype(F32), other[sl, :].astype(F32)
        a_mine, a_other = mine[al, :].astype(F32), other[al, :].astype(F32)
        zero = jnp.zeros_like(s_mine)
        add_s = jnp.where(upper, before[h : h + 1, :] * s_other, zero)
        add_a = jnp.where(upper, zero, after[h : h + 1, :] * a_other)
        if first:
            kept[sl, :] = add_s
            kept[al, :] = add_a
        else:
            kept[sl, :] = held[sl, :] + add_s
            kept[al, :] = held[al, :] + add_a
        low_s, high_s = jnp.where(upper, s_other, s_mine), jnp.where(upper, s_mine, s_other)
        low_a, high_a = jnp.where(upper, a_other, a_mine), jnp.where(upper, a_mine, a_other)
        s_new = high_fade[h : h + 1, :] * low_s + high_s
        a_new = low_fade[h : h + 1, :] * high_a + low_a
        if last:
            sent[sl, :] = jnp.where(next_upper, a_new, s_new).astype(BF16)
        else:
            sent[sl, :] = s_new.astype(BF16)
            sent[al, :] = a_new.astype(BF16)
    kept[2 * cols : 2 * cols + 16, :] = log_before + jnp.where(upper, log_other, 0.0)
    kept[2 * cols + 16 :, :] = log_after + jnp.where(upper, 0.0, log_other)
    if not last:
        log_new = log_mine + log_other
        top = log_new.astype(BF16)
        sent[2 * cols : 2 * cols + 16, :] = top
        sent[2 * cols + 16 :, :] = (log_new - top.astype(F32)).astype(BF16)


def entry_kernel(heads, bit, msg, held, other, st):
    cols = other.shape[0]
    width = cols // heads
    upper = (lax.axis_index("seq") & bit) != 0
    ends = jnp.exp(decay_of(msg, cols))
    before = jnp.exp(held[2 * cols : 2 * cols + 16, :])
    after = jnp.exp(held[2 * cols + 16 :, :])
    for h in range(heads):
        sl = slice(h * width, (h + 1) * width)
        al = slice(cols + h * width, cols + (h + 1) * width)
        far = other[sl, :].astype(F32)
        zero = jnp.zeros_like(far)
        s = held[sl, :] + jnp.where(upper, before[h : h + 1, :] * far, zero)
        a = held[al, :] + jnp.where(upper, zero, after[h : h + 1, :] * far)
        st[sl, :] = s.astype(BF16)
        st[al, :] = (a * ends[h : h + 1, :]).astype(BF16)


def ssm_kernel(masks, gain, *refs):
    count = len(masks)
    uv, st = refs[:count], refs[count : 2 * count]
    b, c, x, g, ew, y, xg, bg, cg, uv_all, st_all = refs[2 * count :]
    rows, cols = x.shape
    heads = gain.shape[0]
    lane = lax.broadcasted_iota(jnp.int32, (1, cols), 1)
    gains = jnp.full((1, cols), gain[0], F32)
    for h in range(1, heads):
        gains = jnp.where(lane >= h * (cols // heads), gain[h], gains)
    me = lax.axis_index("head")
    for j in range(count):
        uv_all[me ^ masks[j]] = uv[j][...]
        st_all[me ^ masks[j]] = st[j][...]
    across = lax.broadcasted_iota(jnp.int32, (rows, rows), 1)
    down = lax.broadcasted_iota(jnp.int32, (rows, rows), 0)
    causal, anti = across <= down, down <= across
    b_rows, c_rows = b[...], c[...]
    near = jnp.where(causal, mm_nt(c_rows, b_rows), 0.0).astype(BF16)
    near_t = jnp.where(anti, mm_nt(b_rows, c_rows), 0.0).astype(BF16)
    out = mm(near, uv[0][:rows, :]) + mm_nt(c_rows, st[0][:cols, :])
    y[...] = (ew[:rows, :] * out + gains * x[...].astype(F32)).astype(BF16)
    back = mm(near_t, uv[0][rows:, :]) + mm_nt(b_rows, st[0][cols:, :])
    xg[...] = (ew[rows:, :] * back + gains * g[...].astype(F32)).astype(BF16)
    slope = jnp.zeros((rows, rows), F32)
    slope_t = jnp.zeros((rows, rows), F32)
    b_sum = jnp.zeros(bg.shape, F32)
    c_sum = jnp.zeros(cg.shape, F32)
    for j in range(count):
        u, w = uv_all[j, :rows, :], uv_all[j, rows:, :]
        slope = slope + mm_nt(w, u)
        slope_t = slope_t + mm_nt(u, w)
        c_sum = c_sum + mm(w, st_all[j, :cols, :])
        b_sum = b_sum + mm(u, st_all[j, cols:, :])
    slope = jnp.where(causal, slope, 0.0).astype(BF16)
    slope_t = jnp.where(anti, slope_t, 0.0).astype(BF16)
    cg[...] = mm(slope, b_rows) + c_sum
    bg[...] = mm(slope_t, c_rows) + b_sum


def starts_of(lengths, pos):
    def lap(j, carry):
        start, at = carry
        return jnp.where(pos >= at, at, start), at + lengths[j]

    docs = lengths.shape[0]
    return lax.fori_loop(0, docs, lap, (jnp.zeros_like(pos), jnp.int32(0)), unroll=docs <= 8)[0]


def forward_kernel(lengths, qg, kv, kv1, kv2, out, dq, stats):
    rows = qg.shape[0] // 2
    base = lax.axis_index("seq") * rows
    pos = base + lax.broadcasted_iota(jnp.int32, (rows, HEAD_DIM), 0)
    start = starts_of(lengths, pos) - base
    start = jnp.concatenate([start] * (rows // HEAD_DIM), axis=1)
    key = lax.broadcasted_iota(jnp.int32, (rows, rows), 1)
    query = lax.broadcasted_iota(jnp.int32, (rows, rows), 0)
    masks = [(key >= start) & (key <= query)]
    masks += [key - d * rows >= start for d in (1, 2)]
    lane = lax.broadcasted_iota(jnp.int32, (rows, HEAD_DIM), 1)
    heads = qg.shape[1] // HEAD_DIM
    collected = jnp.zeros((rows, HEAD_DIM), F32)
    for h in range(heads):
        sl = slice(h * HEAD_DIM, (h + 1) * HEAD_DIM)
        qh, gh = qg[:rows, sl], qg[rows:, sl]
        keys = [r[:rows, sl] for r in (kv, kv1, kv2)]
        values = [r[rows:, sl] for r in (kv, kv1, kv2)]
        scores = [
            jnp.where(m, mm_nt(qh, kk) * SCALE_LOG2E, HIDDEN) for m, kk in zip(masks, keys)
        ]
        top = functools.reduce(jnp.maximum, scores)
        top = jnp.max(top, axis=1, keepdims=True)
        parts = [jnp.exp2(s - top) for s in scores]
        total = jnp.sum(functools.reduce(jnp.add, parts), axis=1, keepdims=True)
        inverse = 1.0 / total
        probs = [p * inverse for p in parts]
        low = [p.astype(BF16) for p in probs]
        rows_out = functools.reduce(jnp.add, [mm(p, vv) for p, vv in zip(low, values)])
        rows_out = rows_out.astype(BF16)
        out[:, sl] = rows_out
        delta = jnp.sum(gh.astype(F32) * rows_out.astype(F32), axis=1, keepdims=True)
        slopes = [
            (p * (mm_nt(gh, vv) - delta)).astype(BF16) for p, vv in zip(probs, values)
        ]
        grad = functools.reduce(jnp.add, [mm(s, kk) for s, kk in zip(slopes, keys)])
        dq[:, sl] = (grad * SCALE).astype(BF16)
        level = top + jnp.log2(total)
        collected = jnp.where(lane == h, level, collected)
        collected = jnp.where(lane == heads + h, delta, collected)
    stats[...] = jnp.transpose(collected)[: stats.shape[0], :]


def backward_kernel(lengths, kv, qg, qg1, qg2, s0, s1, s2, dk, dv):
    rows = kv.shape[0] // 2
    base = lax.axis_index("seq") * rows
    key = lax.broadcasted_iota(jnp.int32, (rows, rows), 0)
    query = lax.broadcasted_iota(jnp.int32, (rows, rows), 1)
    masks = []
    for d in range(REACH + 1):
        pos = base + d * rows + lax.broadcasted_iota(jnp.int32, (8, rows), 1)
        start = (starts_of(lengths, pos) - base)[:1, :]
        mask = key >= start
        masks.append(mask & (key <= query) if d == 0 else mask)
    heads = kv.shape[1] // HEAD_DIM
    for h in range(heads):
        sl = slice(h * HEAD_DIM, (h + 1) * HEAD_DIM)
        kh, vh = kv[:rows, sl], kv[rows:, sl]
        key_sum = value_sum = None
        for mask, far, st in zip(masks, (qg, qg1, qg2), (s0, s1, s2)):
            qh, gh = far[:rows, sl], far[rows:, sl]
            scores = jnp.where(mask, mm_nt(kh, qh) * SCALE_LOG2E - st[h : h + 1, :], HIDDEN)
            probs = jnp.exp2(scores)
            slope = probs * (mm_nt(vh, gh) - st[heads + h : heads + h + 1, :])
            key_part = mm(slope.astype(BF16), qh)
            value_part = mm(probs.astype(BF16), gh)
            key_sum = key_part if key_sum is None else key_sum + key_part
            value_sum = value_part if value_sum is None else value_sum + value_part
        dk[:, sl] = (key_sum * SCALE).astype(BF16)
        dv[:, sl] = value_sum.astype(BF16)


def on_device(
    queries,
    key_rows,
    value_rows,
    attn_out_grad,
    ssm_input,
    b_matrix,
    c_matrix,
    step_sizes,
    decay_rates,
    skip_gain,
    ssm_out_grad,
    doc_lengths,
):
    rows, att_cols = queries.shape
    cols = ssm_input.shape[1]
    n = b_matrix.shape[1]
    heads = step_sizes.shape[1]
    seq_size, head_size = lax.axis_size("seq"), lax.axis_size("head")
    kv, qg, uv, msg, ew = call(
        first_kernel,
        [
            ((2 * rows, att_cols), BF16),
            ((2 * rows, att_cols), BF16),
            ((2 * rows, cols), BF16),
            ((2 * cols + 32, n), BF16),
            ((2 * rows, cols), F32),
        ],
        [SMEM] + [VMEM] * 9,
        "first",
        10**8,
        decay_rates,
        queries,
        key_rows,
        value_rows,
        attn_out_grad,
        ssm_input,
        ssm_out_grad,
        b_matrix,
        c_matrix,
        step_sizes,
    )
    kv1, kv2 = shifted(kv, "seq", 1), shifted(kv, "seq", 2)
    qg1, qg2 = shifted(qg, "seq", -1), shifted(qg, "seq", -2)

    def spread(block):
        blocks, masks, bit = [block], [0], head_size // 2
        while bit:
            blocks = blocks + [swapped(one, "head", bit) for one in blocks]
            masks = masks + [m ^ bit for m in masks]
            bit //= 2
        return blocks, masks

    uvs, masks = spread(uv)
    held, sent, bit = None, msg, 1
    while 2 * bit < seq_size:
        last = 4 * bit >= seq_size
        other = swapped(sent, "seq", bit)
        first = held is None
        sent, held = call(
            functools.partial(join_kernel, heads, bit, first, last),
            [((cols if last else 2 * cols + 32, n), BF16), ((2 * cols + 32, n), F32)],
            [VMEM] * (2 if first else 3),
            f"join{bit}",
            10**6,
            *((sent, other) if first else (sent, other, held)),
        )
        bit *= 2
    other = swapped(sent, "seq", bit)
    (st,) = call(
        functools.partial(entry_kernel, heads, bit),
        [((2 * cols, n), BF16)],
        [VMEM] * 3,
        "entry",
        10**6,
        msg,
        held,
        other,
    )
    sts, _ = spread(st)
    attn_out, query_grad, s0 = call(
        forward_kernel,
        [((rows, att_cols), BF16), ((rows, att_cols), BF16), ((8, rows), F32)],
        [SMEM] + [VMEM] * 4,
        "forward",
        10**9,
        doc_lengths,
        qg,
        kv,
        kv1,
        kv2,
    )
    s1, s2 = shifted(s0, "seq", -1), shifted(s0, "seq", -2)
    key_grad, value_grad = call(
        backward_kernel,
        [((rows, att_cols), BF16), ((rows, att_cols), BF16)],
        [SMEM] + [VMEM] * 7,
        "backward",
        10**9,
        doc_lengths,
        kv,
        qg,
        qg1,
        qg2,
        s0,
        s1,
        s2,
    )
    ssm_out, input_grad, b_grad, c_grad = call(
        functools.partial(ssm_kernel, tuple(masks)),
        [((rows, cols), BF16), ((rows, cols), BF16), ((rows, n), F32), ((rows, n), F32)],
        [SMEM] + [VMEM] * (2 * head_size + 5),
        "ssm",
        10**9,
        skip_gain,
        *uvs,
        *sts,
        b_matrix,
        c_matrix,
        ssm_input,
        ssm_out_grad,
        ew,
        scratch=(
            pltpu.VMEM((head_size, 2 * rows, cols), BF16),
            pltpu.VMEM((head_size, 2 * cols, n), BF16),
        ),
    )
    return (attn_out, query_grad, key_grad, value_grad, ssm_out, input_grad, b_grad, c_grad)


def solution(mesh):
    wide, narrow = P("seq", "head"), P("seq", None)
    return jax.shard_map(
        on_device,
        mesh=mesh,
        in_specs=(wide,) * 5 + (narrow, narrow, wide, P("head"), P("head"), wide, P()),
        out_specs=(wide,) * 6 + (narrow, narrow),
        check_vma=False,
    )
```

time: 176 us -> 68.4 us (0.39)
  local copies, waits for them, and re-layouts: 38.2 us -> 4.17 us
  blocking collectives: 27.2 us -> 0 us
  waiting for transfers between devices: 44.4 us -> 20.2 us
  Pallas kernels: 0 us -> 18.9 us
  between operations: 17 us -> 0.83 us
  matrix products: 14.3 us -> 0 us
  other arithmetic: 14.2 us -> 0 us
  starting transfers between devices: 20.8 us -> 24 us
    psum x1 -> x0, waiting for transfers between devices: 35.4 us -> none  [ssm_layer(): b_grad, c_grad = lax.psum((b_grad, c_grad), 'head')]
    all_gather x1 -> x0, blocking collectives: 27.2 us -> none  [entering(): pieces = jax.tree.map(lambda part: lax.all_gather(part, axis), value)]
    pallas_call x0 -> x7, Pallas kernels: none -> 18.9 us  [call(): pl.pallas_call(kernel, out_shape=[jax.ShapeDtypeStruct(s, d) for s, d in...]
    dot_general x18 -> x0, matrix products: 14.3 us -> none  [the longest x3 2.92 us: ssm_parts(): jnp.einsum('hts,shp->thp', mixing, x_heads, precision=lax.Precision.HIGHEST)]
    ppermute x8 -> x15, waiting for transfers between devices: 8.9 us -> 20.2 us  [the longest x6 10.6 us: shifted(): lax.ppermute(x, axis, [(i, i + by) for i in range(length) if 0 <= i + by...]
    mul x14 -> x0, local copies, waits for them, and re-layouts: 9.66 us -> none  [chained(): later_item[0][:, None, None] * earlier[1] + later_item[1]]
    select_n x14 -> x0, other arithmetic: 8.04 us -> none  [lap(): jnp.where(position < mine, new, old)]
    unnamed x69 -> x37, local copies, waits for them, and re-layouts: 11.9 us -> 4.17 us
  transfers between devices with their start and end apart: 11 -> 15, of which waited for: 2 -> 5; matrix products, arithmetic and copies ran while one was open for 24% -> 0% of each run, Pallas kernels for 0% -> 16%
where the time goes in v1:
time: 68.4 us; the launch traced here: 68 us
  starting transfers between devices  24 us (35%)
  waiting for transfers between devices  20.2 us (30%)
  Pallas kernels  18.9 us (28%)
  local copies, waits for them, and re-layouts  4.17 us (6%)
  between operations  0.83 us (1%)
    pallas_call x7, Pallas kernels, call(): pl.pallas_call(kernel, out_shape=[jax.ShapeDtypeStruct(s, d) for s, d in...  18.9 us
    ppermute x9, starting transfers between devices, swapped(): lax.ppermute(x, axis, [(i, i ^ bit) for i in range(lax.axis_size(axis))])  13.1 us
    ppermute x6, starting transfers between devices, shifted(): lax.ppermute(x, axis, [(i, i + by) for i in range(length) if 0 <= i + by...  10.9 us
    ppermute x6, waiting for transfers between devices, shifted(): lax.ppermute(x, axis, [(i, i + by) for i in range(length) if 0 <= i + by...  10.6 us
    ppermute x9, waiting for transfers between devices, swapped(): lax.ppermute(x, axis, [(i, i ^ bit) for i in range(lax.axis_size(axis))])  9.55 us
    unnamed x37, local copies, waits for them, and re-layouts  4.17 us
  transfers between devices with their start and end apart: 15, of which 5 were waited for; matrix products, arithmetic and copies ran while one was open for 0% of the time, Pallas kernels for 16%

profile of v1, /device:TPU:0, one launch (start us, length us, event | category | flops | bytes accessed | tf_op | source)
XLA Modules:
  0.0 68.0 jit_solution(4601662340065160032)
XLA Ops:
  0.6 1.5 %copy.20.dt = f32[256,2]{1,0:T(8,128)} copy(f32[256,2]{0,1:T(2,128)} %param.19) | data formatting | bytes 4096 | tf_op args[7]
  2.1 2.9 %first.1 = (bf16[512,256]{1,0:T(8,128)(2,1)}, bf16[512,256]{1,0:T(8,128)(2,1)}, bf16[512,128]{1,0:T(8,128)(2,1)}, bf16[288,256]{1,0:T(8,128)(2,1)}, f32[512,128]{1,0:T(8,128)}) custom-call(f32[2]{0:T(128)} %rate.1, bf16[256,256]{1,0:T(8,128)(2,1)} %q.1, bf16[256,256]{1,0:T(8,128)(2,1)} %k.1, bf16[256,256]{1,0:T(8,128)(2,1)} %v.1, bf16[256,256]{1,0:T(8,128)(2,1)} %do.1, ...), custom_call_target="tpu_custom_call" | custom-call | flops 100000000 | bytes 1984520 | tf_op jit(solution)/shard_map/first/pallas_call | solution.py:38
  5.0 3.0 %collective-permute-start.9 = (bf16[288,256]{1,0:T(8,128)(2,1)}, bf16[288,256]{1,0:T(8,128)(2,1)S(1)}, u32[]{:S(2)}, u32[]{:S(2)}) collective-permute-start(bf16[288,256]{1,0:T(8,128)(2,1)} %get-tuple-element.34.mine.msg), channel_id=1, source_target_pairs={{0,4},{4,0},{8,12},{12,8},{16,20},{20,16},{24,28},{28,24},{1,5},{5... | collective-permute-start | bytes 442376 | tf_op jit(solution)/shard_map/ppermute | solution.py:55
  8.0 4.1 %collective-permute-done.9.other = bf16[288,256]{1,0:T(8,128)(2,1)S(1)} collective-permute-done((bf16[288,256]{1,0:T(8,128)(2,1)}, bf16[288,256]{1,0:T(8,128)(2,1)S(1)}, u32[]{:S(2)}, u32[]{:S(2)}) %collective-permute-start.9) | collective-permute-done | bytes 147488 | tf_op jit(solution)/shard_map/ppermute | solution.py:55
  12.0 0.7 copy-done
  12.7 1.8 %join1.1 = (bf16[288,256]{1,0:T(8,128)(2,1)}, f32[288,256]{1,0:T(8,128)}) custom-call(bf16[288,256]{1,0:T(8,128)(2,1)} %get-tuple-element.34.mine.msg, bf16[288,256]{1,0:T(8,128)(2,1)} %copy-done), custom_call_target="tpu_custom_call" | custom-call | flops 1000000 | bytes 737280 | tf_op jit(solution)/shard_map/join1/pallas_call | solution.py:38
  14.5 1.8 %collective-permute-start.10 = (bf16[288,256]{1,0:T(8,128)(2,1)}, bf16[288,256]{1,0:T(8,128)(2,1)S(1)}, u32[]{:S(2)}, u32[]{:S(2)}) collective-permute-start(bf16[288,256]{1,0:T(8,128)(2,1)} %get-tuple-element.35.mine), channel_id=1, source_target_pairs={{0,8},{4,12},{8,0},{12,4},{16,24},{20,28},{24,16},{28,20},{1,9},{5... | collective-permute-start | bytes 442376 | tf_op jit(solution)/shard_map/ppermute | solution.py:55
  16.3 3.4 %collective-permute-start = (bf16[512,256]{1,0:T(8,128)(2,1)S(1)}, bf16[512,256]{1,0:T(8,128)(2,1)S(1)}, u32[]{:S(2)}, u32[]{:S(2)}) collective-permute-start(bf16[512,256]{1,0:T(8,128)(2,1)S(1)} %copy-done.3), channel_id=1, source_target_pairs={{0,4},{4,8},{8,12},{12,16},{16,20},{20,24},{24,28},{1,5},{5,9},{9,... | collective-permute-start | bytes 786440 | tf_op jit(solution)/shard_map/ppermute | solution.py:51
  19.8 2.4 %collective-permute-start.1 = (bf16[512,256]{1,0:T(8,128)(2,1)S(1)}, bf16[512,256]{1,0:T(8,128)(2,1)S(1)}, u32[]{:S(2)}, u32[]{:S(2)}) collective-permute-start(bf16[512,256]{1,0:T(8,128)(2,1)S(1)} %copy-done.3), channel_id=1, source_target_pairs={{0,8},{4,12},{8,16},{12,20},{16,24},{20,28},{1,9},{5,13},{9,17},{1... | collective-permute-start | bytes 786440 | tf_op jit(solution)/shard_map/ppermute | solution.py:51
  22.1 1.3 %collective-permute-start.2 = (bf16[512,256]{1,0:T(8,128)(2,1)}, bf16[512,256]{1,0:T(8,128)(2,1)S(1)}, u32[]{:S(2)}, u32[]{:S(2)}) collective-permute-start(bf16[512,256]{1,0:T(8,128)(2,1)} %get-tuple-element.26.qg), channel_id=1, source_target_pairs={{4,0},{8,4},{12,8},{16,12},{20,16},{24,20},{28,24},{5,1},{9,5},{13... | collective-permute-start | bytes 786440 | tf_op jit(solution)/shard_map/ppermute | solution.py:51
  23.4 1.6 %collective-permute-start.6 = (bf16[512,128]{1,0:T(8,128)(2,1)}, bf16[512,128]{1,0:T(8,128)(2,1)S(1)}, u32[]{:S(2)}, u32[]{:S(2)}) collective-permute-start(bf16[512,128]{1,0:T(8,128)(2,1)} %get-tuple-element.33.refs_0_), channel_id=1, source_target_pairs={{0,2},{1,3},{2,0},{3,1},{4,6},{5,7},{6,4},{7,5},{8,10},{9,11},{10,... | collective-permute-start | bytes 393224 | tf_op jit(solution)/shard_map/ppermute | solution.py:55
  25.0 0.7 copy-done.1
  25.7 2.0 %join2.1 = (bf16[128,256]{1,0:T(8,128)(2,1)}, f32[288,256]{1,0:T(8,128)}) custom-call(bf16[288,256]{1,0:T(8,128)(2,1)} %get-tuple-element.35.mine, bf16[288,256]{1,0:T(8,128)(2,1)} %copy-done.1, f32[288,256]{1,0:T(8,128)} %get-tuple-element.36.refs_0_), custom_call_target="tpu_custom_call" | custom-call | flops 1000000 | bytes 950272 | tf_op jit(solution)/shard_map/join2/pallas_call | solution.py:38
  27.6 4.6 %collective-permute-start.11 = (bf16[128,256]{1,0:T(8,128)(2,1)}, bf16[128,256]{1,0:T(8,128)(2,1)S(1)}, u32[]{:S(2)}, u32[]{:S(2)}) collective-permute-start(bf16[128,256]{1,0:T(8,128)(2,1)} %get-tuple-element.38), channel_id=1, source_target_pairs={{0,16},{4,20},{8,24},{12,28},{16,0},{20,4},{24,8},{28,12},{1,17},{... | collective-permute-start | bytes 196616 | tf_op jit(solution)/shard_map/ppermute | solution.py:55
  32.2 2.5 %collective-permute-done.11.other = bf16[128,256]{1,0:T(8,128)(2,1)S(1)} collective-permute-done((bf16[128,256]{1,0:T(8,128)(2,1)}, bf16[128,256]{1,0:T(8,128)(2,1)S(1)}, u32[]{:S(2)}, u32[]{:S(2)}) %collective-permute-start.11) | collective-permute-done | bytes 65568 | tf_op jit(solution)/shard_map/ppermute | solution.py:55
  34.7 1.3 %collective-permute-start.3 = (bf16[512,256]{1,0:T(8,128)(2,1)S(1)}, bf16[512,256]{1,0:T(8,128)(2,1)S(1)}, u32[]{:S(2)}, u32[]{:S(2)}) collective-permute-start(bf16[512,256]{1,0:T(8,128)(2,1)S(1)} %copy-done.4), channel_id=1, source_target_pairs={{8,0},{12,4},{16,8},{20,12},{24,16},{28,20},{9,1},{13,5},{17,9},{2... | collective-permute-start | bytes 786440 | tf_op jit(solution)/shard_map/ppermute | solution.py:51
  36.0 1.7 %entry.1.refs_4_ = bf16[256,256]{1,0:T(8,128)(2,1)} custom-call(bf16[288,256]{1,0:T(8,128)(2,1)} %get-tuple-element.34.mine.msg, f32[288,256]{1,0:T(8,128)} %get-tuple-element.37.held, bf16[128,256]{1,0:T(8,128)(2,1)} %copy-done.2), custom_call_target="tpu_custom_call" | custom-call | flops 1000000 | bytes 638976 | tf_op jit(solution)/shard_map/entry/pallas_call | solution.py:38
  37.8 1.5 %collective-permute-start.12 = (bf16[256,256]{1,0:T(8,128)(2,1)}, bf16[256,256]{1,0:T(8,128)(2,1)S(1)}, u32[]{:S(2)}, u32[]{:S(2)}) collective-permute-start(bf16[256,256]{1,0:T(8,128)(2,1)} %entry.1.refs_4_), channel_id=1, source_target_pairs={{0,2},{1,3},{2,0},{3,1},{4,6},{5,7},{6,4},{7,5},{8,10},{9,11},{10,... | collective-permute-start | bytes 393224 | tf_op jit(solution)/shard_map/ppermute | solution.py:55
  39.2 0.1 collective-permute-start.7
  39.3 0.5 collective-permute-start.8
  39.8 0.1 collective-permute-start.13
  39.9 3.0 %collective-permute-done.12.refs_5_ = bf16[256,256]{1,0:T(8,128)(2,1)S(1)} collective-permute-done((bf16[256,256]{1,0:T(8,128)(2,1)}, bf16[256,256]{1,0:T(8,128)(2,1)S(1)}, u32[]{:S(2)}, u32[]{:S(2)}) %collective-permute-start.12) | collective-permute-done | bytes 131104 | tf_op jit(solution)/shard_map/ppermute | solution.py:55
  43.0 3.8 %forward.1 = (bf16[256,256]{1,0:T(8,128)(2,1)}, bf16[256,256]{1,0:T(8,128)(2,1)}, f32[8,256]{1,0:T(8,128)}) custom-call(s32[8]{0:T(128)} %lengths.3, bf16[512,256]{1,0:T(8,128)(2,1)} %get-tuple-element.26.qg, bf16[512,256]{1,0:T(8,128)(2,1)} %get-tuple-element.27.kv, bf16[512,256]{1,0:T(8,128)(2,1)} %copy-done.6, bf16[512,256]{1,0:T(8,128)(2,1)} %copy-done.7), custom_call_target="tpu_custom_call" | custom-call | flops 1000000000 | bytes 1318944 | tf_op jit(solution)/shard_map/forward/pallas_call | solution.py:38
  46.8 1.3 %collective-permute-start.4 = (f32[8,256]{1,0:T(8,128)}, f32[8,256]{1,0:T(8,128)S(1)}, u32[]{:S(2)}, u32[]{:S(2)}) collective-permute-start(f32[8,256]{1,0:T(8,128)} %get-tuple-element.30.s0), channel_id=1, source_target_pairs={{4,0},{8,4},{12,8},{16,12},{20,16},{24,20},{28,24},{5,1},{9,5},{13... | collective-permute-start | bytes 24584 | tf_op jit(solution)/shard_map/ppermute | solution.py:51
  48.1 4.5 %collective-permute-done.4.s1 = f32[8,256]{1,0:T(8,128)S(1)} collective-permute-done((f32[8,256]{1,0:T(8,128)}, f32[8,256]{1,0:T(8,128)S(1)}, u32[]{:S(2)}, u32[]{:S(2)}) %collective-permute-start.4) | collective-permute-done | bytes 8224 | tf_op jit(solution)/shard_map/ppermute | solution.py:51
  52.6 1.3 %collective-permute-start.5 = (f32[8,256]{1,0:T(8,128)}, f32[8,256]{1,0:T(8,128)S(1)}, u32[]{:S(2)}, u32[]{:S(2)}) collective-permute-start(f32[8,256]{1,0:T(8,128)} %get-tuple-element.30.s0), channel_id=1, source_target_pairs={{8,0},{12,4},{16,8},{20,12},{24,16},{28,20},{9,1},{13,5},{17,9},{2... | collective-permute-start | bytes 24584 | tf_op jit(solution)/shard_map/ppermute | solution.py:51
  53.8 6.1 %collective-permute-done.5.s2 = f32[8,256]{1,0:T(8,128)S(1)} collective-permute-done((f32[8,256]{1,0:T(8,128)}, f32[8,256]{1,0:T(8,128)S(1)}, u32[]{:S(2)}, u32[]{:S(2)}) %collective-permute-start.5) | collective-permute-done | bytes 8224 | tf_op jit(solution)/shard_map/ppermute | solution.py:51
  60.0 0.6 copy-done.17
  60.6 3.3 %backward.1 = (bf16[256,256]{1,0:T(8,128)(2,1)}, bf16[256,256]{1,0:T(8,128)(2,1)}) custom-call(s32[8]{0:T(128)} %lengths.3, bf16[512,256]{1,0:T(8,128)(2,1)} %get-tuple-element.27.kv, bf16[512,256]{1,0:T(8,128)(2,1)} %get-tuple-element.26.qg, bf16[512,256]{1,0:T(8,128)(2,1)} %copy-done.5, bf16[512,256]{1,0:T(8,128)(2,1)} %copy-done.8, ...), custom_call_target="tpu_custom_call" | custom-call | flops 1000000000 | bytes 1335328 | tf_op jit(solution)/shard_map/backward/pallas_call | solution.py:38
  63.9 0.6 copy-done.12
  64.6 0.1 copy-done.14
  64.7 3.3 %ssm.1 = (bf16[256,128]{1,0:T(8,128)(2,1)}, bf16[256,128]{1,0:T(8,128)(2,1)}, f32[256,256]{1,0:T(8,128)}, f32[256,256]{1,0:T(8,128)}) custom-call(f32[2]{0:T(128)} %gain.1, bf16[512,128]{1,0:T(8,128)(2,1)} %get-tuple-element.33.refs_0_, bf16[512,128]{1,0:T(8,128)(2,1)} %copy-done.10, bf16[512,128]{1,0:T(8,128)(2,1)} %copy-done.12, ...), custom_call_target="tpu_custom_call" | custom-call | flops 1000000000 | bytes 2359304 | tf_op jit(solution)/shard_map/ssm/pallas_call | solution.py:38
  (42 shorter events, 0.1 us)
Async XLA Ops:
  5.0 11.3 %copy-start.3 = (bf16[512,256]{1,0:T(8,128)(2,1)S(1)}, bf16[512,256]{1,0:T(8,128)(2,1)}, u32[]{:S(2)}) copy-start(bf16[512,256]{1,0:T(8,128)(2,1)} %get-tuple-element.27.kv) | copy-start | bytes 786436
  5.0 7.0 %collective-permute-start.9 = (bf16[288,256]{1,0:T(8,128)(2,1)}, bf16[288,256]{1,0:T(8,128)(2,1)S(1)}, u32[]{:S(2)}, u32[]{:S(2)}) collective-permute-start(bf16[288,256]{1,0:T(8,128)(2,1)} %get-tuple-element.34.mine.msg), channel_id=1, source_target_pairs={{0,4},{4,0},{8,12},{12,8},{16,20},{20,16},{24,28},{28,24},{1,5},{5... | collective-permute-start | bytes 442376 | tf_op jit(solution)/shard_map/ppermute | solution.py:55
  12.0 0.7 copy-start
  14.5 10.5 %collective-permute-start.10 = (bf16[288,256]{1,0:T(8,128)(2,1)}, bf16[288,256]{1,0:T(8,128)(2,1)S(1)}, u32[]{:S(2)}, u32[]{:S(2)}) collective-permute-start(bf16[288,256]{1,0:T(8,128)(2,1)} %get-tuple-element.35.mine), channel_id=1, source_target_pairs={{0,8},{4,12},{8,0},{12,4},{16,24},{20,28},{24,16},{28,20},{1,9},{5... | collective-permute-start | bytes 442376 | tf_op jit(solution)/shard_map/ppermute | solution.py:55
  16.3 22.9 %collective-permute-start = (bf16[512,256]{1,0:T(8,128)(2,1)S(1)}, bf16[512,256]{1,0:T(8,128)(2,1)S(1)}, u32[]{:S(2)}, u32[]{:S(2)}) collective-permute-start(bf16[512,256]{1,0:T(8,128)(2,1)S(1)} %copy-done.3), channel_id=1, source_target_pairs={{0,4},{4,8},{8,12},{12,16},{16,20},{20,24},{24,28},{1,5},{5,9},{9,... | collective-permute-start | bytes 786440 | tf_op jit(solution)/shard_map/ppermute | solution.py:51
  19.8 19.5 %collective-permute-start.1 = (bf16[512,256]{1,0:T(8,128)(2,1)S(1)}, bf16[512,256]{1,0:T(8,128)(2,1)S(1)}, u32[]{:S(2)}, u32[]{:S(2)}) collective-permute-start(bf16[512,256]{1,0:T(8,128)(2,1)S(1)} %copy-done.3), channel_id=1, source_target_pairs={{0,8},{4,12},{8,16},{12,20},{16,24},{20,28},{1,9},{5,13},{9,17},{1... | collective-permute-start | bytes 786440 | tf_op jit(solution)/shard_map/ppermute | solution.py:51
  22.1 17.7 %collective-permute-start.2 = (bf16[512,256]{1,0:T(8,128)(2,1)}, bf16[512,256]{1,0:T(8,128)(2,1)S(1)}, u32[]{:S(2)}, u32[]{:S(2)}) collective-permute-start(bf16[512,256]{1,0:T(8,128)(2,1)} %get-tuple-element.26.qg), channel_id=1, source_target_pairs={{4,0},{8,4},{12,8},{16,12},{20,16},{24,20},{28,24},{5,1},{9,5},{13... | collective-permute-start | bytes 786440 | tf_op jit(solution)/shard_map/ppermute | solution.py:51
  23.4 14.3 %collective-permute-start.6 = (bf16[512,128]{1,0:T(8,128)(2,1)}, bf16[512,128]{1,0:T(8,128)(2,1)S(1)}, u32[]{:S(2)}, u32[]{:S(2)}) collective-permute-start(bf16[512,128]{1,0:T(8,128)(2,1)} %get-tuple-element.33.refs_0_), channel_id=1, source_target_pairs={{0,2},{1,3},{2,0},{3,1},{4,6},{5,7},{6,4},{7,5},{8,10},{9,11},{10,... | collective-permute-start | bytes 393224 | tf_op jit(solution)/shard_map/ppermute | solution.py:55
  25.0 0.7 copy-start.1
  25.7 9.0 %copy-start.4 = (bf16[512,256]{1,0:T(8,128)(2,1)S(1)}, bf16[512,256]{1,0:T(8,128)(2,1)}, u32[]{:S(2)}) copy-start(bf16[512,256]{1,0:T(8,128)(2,1)} %get-tuple-element.26.qg) | copy-start | bytes 786436
  27.6 7.1 %collective-permute-start.11 = (bf16[128,256]{1,0:T(8,128)(2,1)}, bf16[128,256]{1,0:T(8,128)(2,1)S(1)}, u32[]{:S(2)}, u32[]{:S(2)}) collective-permute-start(bf16[128,256]{1,0:T(8,128)(2,1)} %get-tuple-element.38), channel_id=1, source_target_pairs={{0,16},{4,20},{8,24},{12,28},{16,0},{20,4},{24,8},{28,12},{1,17},{... | collective-permute-start | bytes 196616 | tf_op jit(solution)/shard_map/ppermute | solution.py:55
  34.7 1.3 %copy-start.2 = (bf16[128,256]{1,0:T(8,128)(2,1)}, bf16[128,256]{1,0:T(8,128)(2,1)S(1)}, u32[]{:S(2)}) copy-start(bf16[128,256]{1,0:T(8,128)(2,1)S(1)} %collective-permute-done.11.other) | copy-start | bytes 196612
  34.7 12.1 %collective-permute-start.3 = (bf16[512,256]{1,0:T(8,128)(2,1)S(1)}, bf16[512,256]{1,0:T(8,128)(2,1)S(1)}, u32[]{:S(2)}, u32[]{:S(2)}) collective-permute-start(bf16[512,256]{1,0:T(8,128)(2,1)S(1)} %copy-done.4), channel_id=1, source_target_pairs={{8,0},{12,4},{16,8},{20,12},{24,16},{28,20},{9,1},{13,5},{17,9},{2... | collective-permute-start | bytes 786440 | tf_op jit(solution)/shard_map/ppermute | solution.py:51
  36.0 3.2 %copy-start.9 = (bf16[512,128]{1,0:T(8,128)(2,1)S(1)}, bf16[512,128]{1,0:T(8,128)(2,1)}, u32[]{:S(2)}) copy-start(bf16[512,128]{1,0:T(8,128)(2,1)} %get-tuple-element.33.refs_0_) | copy-start | bytes 393220
  37.8 9.0 %copy-start.10 = (bf16[512,128]{1,0:T(8,128)(2,1)}, bf16[512,128]{1,0:T(8,128)(2,1)S(1)}, u32[]{:S(2)}) copy-start(bf16[512,128]{1,0:T(8,128)(2,1)S(1)} %collective-permute-done.6.refs_1_) | copy-start | bytes 393220
  37.8 5.2 %collective-permute-start.12 = (bf16[256,256]{1,0:T(8,128)(2,1)}, bf16[256,256]{1,0:T(8,128)(2,1)S(1)}, u32[]{:S(2)}, u32[]{:S(2)}) collective-permute-start(bf16[256,256]{1,0:T(8,128)(2,1)} %entry.1.refs_4_), channel_id=1, source_target_pairs={{0,2},{1,3},{2,0},{3,1},{4,6},{5,7},{6,4},{7,5},{8,10},{9,11},{10,... | collective-permute-start | bytes 393224 | tf_op jit(solution)/shard_map/ppermute | solution.py:55
  39.2 3.7 %copy-start.6 = (bf16[512,256]{1,0:T(8,128)(2,1)}, bf16[512,256]{1,0:T(8,128)(2,1)S(1)}, u32[]{:S(2)}) copy-start(bf16[512,256]{1,0:T(8,128)(2,1)S(1)} %collective-permute-done.kv1) | copy-start | bytes 786436
  39.2 24.7 %collective-permute-start.7 = (bf16[512,128]{1,0:T(8,128)(2,1)S(1)}, bf16[512,128]{1,0:T(8,128)(2,1)S(1)}, u32[]{:S(2)}, u32[]{:S(2)}) collective-permute-start(bf16[512,128]{1,0:T(8,128)(2,1)S(1)} %copy-done.9), channel_id=1, source_target_pairs={{0,1},{1,0},{2,3},{3,2},{4,5},{5,4},{6,7},{7,6},{8,9},{9,8},{10,11... | collective-permute-start | bytes 393224 | tf_op jit(solution)/shard_map/ppermute | solution.py:55
  39.3 3.6 %copy-start.7 = (bf16[512,256]{1,0:T(8,128)(2,1)}, bf16[512,256]{1,0:T(8,128)(2,1)S(1)}, u32[]{:S(2)}) copy-start(bf16[512,256]{1,0:T(8,128)(2,1)S(1)} %collective-permute-done.1.kv2) | copy-start | bytes 786436
  39.3 24.6 %collective-permute-start.8 = (bf16[512,128]{1,0:T(8,128)(2,1)S(1)}, bf16[512,128]{1,0:T(8,128)(2,1)S(1)}, u32[]{:S(2)}, u32[]{:S(2)}) collective-permute-start(bf16[512,128]{1,0:T(8,128)(2,1)S(1)} %collective-permute-done.6.refs_1_), channel_id=1, source_target_pairs={{0,1},{1,0},{2,3},{3,2},{4,5},{5,4},{6,7},{7,6},{8,9},{9,8},{10,11... | collective-permute-start | bytes 393224 | tf_op jit(solution)/shard_map/ppermute | solution.py:55
  39.8 7.0 %copy-start.5 = (bf16[512,256]{1,0:T(8,128)(2,1)}, bf16[512,256]{1,0:T(8,128)(2,1)S(1)}, u32[]{:S(2)}) copy-start(bf16[512,256]{1,0:T(8,128)(2,1)S(1)} %collective-permute-done.2.qg1) | copy-start | bytes 786436
  39.8 24.1 %collective-permute-start.13 = (bf16[256,256]{1,0:T(8,128)(2,1)}, bf16[256,256]{1,0:T(8,128)(2,1)S(1)}, u32[]{:S(2)}, u32[]{:S(2)}) collective-permute-start(bf16[256,256]{1,0:T(8,128)(2,1)} %entry.1.refs_4_), channel_id=1, source_target_pairs={{0,1},{1,0},{2,3},{3,2},{4,5},{5,4},{6,7},{7,6},{8,9},{9,8},{10,11... | collective-permute-start | bytes 393224 | tf_op jit(solution)/shard_map/ppermute | solution.py:55
  42.9 3.8 %copy-start.11 = (bf16[256,256]{1,0:T(8,128)(2,1)}, bf16[256,256]{1,0:T(8,128)(2,1)S(1)}, u32[]{:S(2)}) copy-start(bf16[256,256]{1,0:T(8,128)(2,1)S(1)} %collective-permute-done.12.refs_5_) | copy-start | bytes 393220
  42.9 21.0 %collective-permute-start.14 = (bf16[256,256]{1,0:T(8,128)(2,1)S(1)}, bf16[256,256]{1,0:T(8,128)(2,1)S(1)}, u32[]{:S(2)}, u32[]{:S(2)}) collective-permute-start(bf16[256,256]{1,0:T(8,128)(2,1)S(1)} %collective-permute-done.12.refs_5_), channel_id=1, source_target_pairs={{0,1},{1,0},{2,3},{3,2},{4,5},{5,4},{6,7},{7,6},{8,9},{9,8},{10,11... | collective-permute-start | bytes 393224 | tf_op jit(solution)/shard_map/ppermute | solution.py:55
  46.8 13.2 %copy-start.8 = (bf16[512,256]{1,0:T(8,128)(2,1)}, bf16[512,256]{1,0:T(8,128)(2,1)S(1)}, u32[]{:S(2)}) copy-start(bf16[512,256]{1,0:T(8,128)(2,1)S(1)} %collective-permute-done.3.qg2) | copy-start | bytes 786436
  46.8 5.8 %collective-permute-start.4 = (f32[8,256]{1,0:T(8,128)}, f32[8,256]{1,0:T(8,128)S(1)}, u32[]{:S(2)}, u32[]{:S(2)}) collective-permute-start(f32[8,256]{1,0:T(8,128)} %get-tuple-element.30.s0), channel_id=1, source_target_pairs={{4,0},{8,4},{12,8},{16,12},{20,16},{24,20},{28,24},{5,1},{9,5},{13... | collective-permute-start | bytes 24584 | tf_op jit(solution)/shard_map/ppermute | solution.py:51
  52.5 7.4 %copy-start.16 = (f32[8,256]{1,0:T(8,128)}, f32[8,256]{1,0:T(8,128)S(1)}, u32[]{:S(2)}) copy-start(f32[8,256]{1,0:T(8,128)S(1)} %collective-permute-done.4.s1) | copy-start | bytes 24580
  52.6 7.4 %collective-permute-start.5 = (f32[8,256]{1,0:T(8,128)}, f32[8,256]{1,0:T(8,128)S(1)}, u32[]{:S(2)}, u32[]{:S(2)}) collective-permute-start(f32[8,256]{1,0:T(8,128)} %get-tuple-element.30.s0), channel_id=1, source_target_pairs={{8,0},{12,4},{16,8},{20,12},{24,16},{28,20},{9,1},{13,5},{17,9},{2... | collective-permute-start | bytes 24584 | tf_op jit(solution)/shard_map/ppermute | solution.py:51
  63.9 0.7 copy-start.12
  63.9 0.7 %copy-start.13 = (bf16[512,128]{1,0:T(8,128)(2,1)}, bf16[512,128]{1,0:T(8,128)(2,1)S(1)}, u32[]{:S(2)}) copy-start(bf16[512,128]{1,0:T(8,128)(2,1)S(1)} %collective-permute-done.8.refs_3_) | copy-start | bytes 393220
  63.9 0.7 %copy-start.14 = (bf16[256,256]{1,0:T(8,128)(2,1)}, bf16[256,256]{1,0:T(8,128)(2,1)S(1)}, u32[]{:S(2)}) copy-start(bf16[256,256]{1,0:T(8,128)(2,1)S(1)} %collective-permute-done.13.refs_6_) | copy-start | bytes 393220
  63.9 0.7 %copy-start.15 = (bf16[256,256]{1,0:T(8,128)(2,1)}, bf16[256,256]{1,0:T(8,128)(2,1)S(1)}, u32[]{:S(2)}) copy-start(bf16[256,256]{1,0:T(8,128)(2,1)S(1)} %collective-permute-done.14.refs_7_) | copy-start | bytes 393220
  (1 other events, 0.6 us)
